TPU v7x, 128 devices: a whole 4x4x4 slice. The times are simulated.
128 devices in a mesh: chan: 2 (over x_hi), blk: 64 (over y, z, x_lo, core).
Axes of the slice: x: 4 (x_hi: 2, x_lo: 2; x = x_hi * 2 + x_lo), y: 4, z: 4, core: 2. Of those that a mesh axis runs over, the one named last changes fastest.
Arguments:
- features: bfloat16 [64, 2, 256, 128], P('blk', 'chan'), may hold values from -6 to 6
- transforms: bfloat16 [8, 128, 128], replicated, may hold values from -0.5 to 0.5
- self_weight: bfloat16 [128, 128], replicated, may hold values from -0.5 to 0.5
- tile_rows: int32 [8, 64, 64, 8], P('chan', 'blk'), may hold values from 0 to 3
- tile_cols: int32 [8, 64, 64, 8], P('chan', 'blk'), may hold values from 0 to 3
- tile_ids: int32 [8, 64, 64, 8], P('chan', 'blk'), may hold values from 0 to 31
- tile_count: int32 [8, 64, 64], P('chan', 'blk'), may hold values from 0 to 8
- tile_pool: bfloat16 [8, 64, 32, 128, 128], P('chan', 'blk'), may hold values from -0.0234375 to 0.0234375
Outputs:
- updated: bfloat16 [64, 2, 256, 128], P('blk', 'chan')
All inputs are finite; a program needn't handle non-finite values.
Results may differ from a plain program's by a relative error of at most 0.0041.
Values may be sent and summed in bfloat16 or wider, within the bound.
No kernel may reach another device: no remote copies, remote signals or barrier semaphores. Data moves between devices by JAX's collectives and lax.ppermute only.
A program may use at most 128 MiB of HBM per device.

v0:
```python
import math
import jax
import jax.numpy as jnp
from jax import lax
from jax.sharding import PartitionSpec as P


def shards(
    features, transforms, self_weight, tile_rows, tile_cols, tile_ids, tile_count, tile_pool
):
    chan_count = lax.axis_size("chan")
    chan_index = lax.axis_index("chan")
    own_rows = features[0, 0]
    half_rows = own_rows.shape[0]
    width = own_rows.shape[1]
    tile_size = tile_pool.shape[-1]
    pool_size = tile_pool.shape[2]
    block_rows = half_rows * chan_count
    tiles_block = block_rows // tile_size
    rel_dev = transforms.shape[0] // chan_count
    slot_count = tile_rows.shape[-1]
    rows_list = tile_rows[:, 0]
    cols_list = tile_cols[:, 0]
    ids_list = tile_ids[:, 0]
    count_list = tile_count[:, 0]
    pool_flat = tile_pool[:, 0].reshape(rel_dev, pool_size, tile_size * tile_size)
    slot_range = jnp.arange(slot_count)
    tile_range = jnp.arange(tiles_block)
    pool_range = jnp.arange(pool_size)

    def apply_group(total, hidden_group, first):
        group = hidden_group.shape[1]
        cols_now = lax.dynamic_slice_in_dim(cols_list, first, group, 1)
        rows_now = lax.dynamic_slice_in_dim(rows_list, first, group, 1)
        ids_now = lax.dynamic_slice_in_dim(ids_list, first, group, 1)
        count_now = lax.dynamic_slice_in_dim(count_list, first, group, 1)
        pick_cols = (cols_now[..., None] == tile_range).astype(jnp.bfloat16)
        flat_hidden = hidden_group.reshape(rel_dev, group, tiles_block, tile_size * width)
        picked = jnp.einsum(
            "rgks,rgsx->rgkx", pick_cols, flat_hidden, preferred_element_type=jnp.float32
        ).astype(jnp.bfloat16)
        picked = picked.reshape(rel_dev, group, slot_count, tile_size, width)
        pick_ids = (ids_now[..., None] == pool_range).astype(jnp.bfloat16)
        weights = jnp.einsum(
            "rgkp,rpx->rgkx", pick_ids, pool_flat, preferred_element_type=jnp.float32
        ).astype(jnp.bfloat16)
        weights = weights.reshape(rel_dev, group, slot_count, tile_size, tile_size)
        product = jnp.einsum(
            "rgkab,rgkbd->rgkad", weights, picked, preferred_element_type=jnp.float32
        )
        live = (slot_range < count_now[..., None]).astype(jnp.float32)
        onehot = (rows_now[..., None] == tile_range).astype(jnp.float32) * live[..., None]
        return total + jnp.einsum(
            "rgkt,rgkad->tad", onehot, product, precision=lax.Precision.HIGHEST
        )

    empty = jnp.zeros((tiles_block, tile_size, width), jnp.float32)
    all_hidden = jnp.einsum(
        "nd,rde->rne", own_rows, transforms, preferred_element_type=jnp.float32
    ).astype(jnp.bfloat16)
    mine = lax.all_to_all(all_hidden, "chan", split_axis=0, concat_axis=1, tiled=True)
    piece = lax.all_gather(mine, "blk", axis=1, tiled=True)
    blocks_here = piece.shape[1] // block_rows

    def fetch(offset, group):
        part_rows = lax.dynamic_slice_in_dim(piece, offset * block_rows, group * block_rows, 1)
        return part_rows.reshape(rel_dev, group, tiles_block, tile_size, width)

    group = math.gcd(blocks_here, 4)
    turns = blocks_here // group

    def step_once(turn, carry):
        return apply_group(carry, fetch(turn * group, group), turn * group)

    agg = lax.fori_loop(0, turns, step_once, empty)
    partial_rows = agg.reshape(block_rows, width)
    summed = lax.psum(partial_rows, "chan")
    share = lax.dynamic_slice_in_dim(summed, chan_index * half_rows, half_rows, 0)
    selfterm = jnp.dot(own_rows, self_weight, preferred_element_type=jnp.float32)
    updated = jax.nn.relu(selfterm + share).astype(jnp.bfloat16)
    return updated.reshape(1, 1, half_rows, width)


def solution(mesh):
    placed = (
        P("blk", "chan", None, None),
        P(),
        P(),
        P("chan", "blk", None, None),
        P("chan", "blk", None, None),
        P("chan", "blk", None, None),
        P("chan", "blk", None),
        P("chan", "blk", None, None, None),
    )
    return jax.shard_map(
        shards, mesh=mesh, in_specs=placed, out_specs=P("blk", "chan", None, None), check_vma=False
    )
```

profile of v0, /device:TPU:1, one launch (start us, length us, event | category | flops | bytes accessed | tf_op | source)
XLA Modules:
  0.0 706.5 jit_solution(2026471395278241592)
XLA Ops:
  8.7 13.2 %all_to_all.18 = bf16[8,256,128]{1,2,0:T(8,128)(2,1)S(1)} all-to-all(bf16[8,256,128]{1,2,0:T(8,128)(2,1)S(1)} %fusion.31), channel_id=1, replica_groups=mesh['chan'=2,'blk'=64] {'chan'}, dimensions={0} | all-to-all | bytes 1048576 | tf_op jit(solution)/shard_map/all_to_all | solution.py:61
  23.0 7.3 %reshape_squeeze.3 = bf16[4,32,16384]{2,1,0:T(8,128)(2,1)} reshape(bf16[4,1,32,128,128]{4,3,2,1,0:T(8,128)(2,1)} %param.17) | data formatting | bytes 8388608 | tf_op jit(solution)/shard_map/reshape;squeeze | solution.py:26
  30.8 181.1 %all-gather.2.cloned.1.call-done = bf16[4,32768,128]{2,1,0:T(8,128)(2,1)} async-done(((bf16[4,512,128]{2,1,0:T(8,128)(2,1)}), bf16[4,32768,128]{2,1,0:T(8,128)(2,1)}) %all-gather.2.cloned.1.call-update) | async-done | bytes 33554448 | tf_op jit(solution)/shard_map/all_gather | solution.py:62
  211.9 453.9 %while.17 = (s32[]{:T(128)}, f32[4,128,128]{2,0,1:T(4,128)S(1)}, s32[4,64,8]{2,0,1:T(4,128)S(1)}, s32[4,64]{0,1:T(8,128)S(1)}, s32[4,64,8]{2,1,0:T(8,128)S(1)}, ...) while((s32[]{:T(128)}, f32[4,128,128]{2,0,1:T(4,128)S(1)}, ...), condition=%wide.region_1.0_spmd.clone.clone, body=%wide.region_0.0_spmd.clone.clone.sunk | while | flops 792860416 | bytes 65542100 | solution.py:75
  211.9 3.1 constant_dynamic-slice_fusion.9
  214.9 2.6 reshape.58
  221.1 4.5 fusion.61
  225.6 14.6 %fusion.63 = f32[4,128,128]{2,0,1:T(4,128)S(1)} fusion(f32[4,4,8,128,128]{4,3,2,1,0:T(8,128)} %fusion.61, f32[4,128,128]{2,0,1:T(4,128)S(1)} %get-tuple-element.418, pred[]{:T(512)S(6)} %compare.3, f32[4,4,8]{2,0,1:T(4,128)S(1)} %fusion.62, s32[4,4,8]{2,0,1:T(4,128)S(1)} %get-tuple-element.402), kind=kOutput, calls=%fused_computation.14.clone.1 | convolution fusion | flops 100795392 | bytes 8913921 | tf_op jit(solution)/shard_map/while/body/eval_jaxpr/rgkt,rgkad->tad/dot_general | solution.py:53
  240.2 3.1 constant_dynamic-slice_fusion.9
  243.3 2.6 reshape.58
  249.4 4.5 fusion.61
  254.0 14.6 %fusion.63 = f32[4,128,128]{2,0,1:T(4,128)S(1)} fusion(f32[4,4,8,128,128]{4,3,2,1,0:T(8,128)} %fusion.61, f32[4,128,128]{2,0,1:T(4,128)S(1)} %get-tuple-element.418, pred[]{:T(512)S(6)} %compare.3, f32[4,4,8]{2,0,1:T(4,128)S(1)} %fusion.62, s32[4,4,8]{2,0,1:T(4,128)S(1)} %get-tuple-element.402), kind=kOutput, calls=%fused_computation.14.clone.1 | convolution fusion | flops 100795392 | bytes 8913921 | tf_op jit(solution)/shard_map/while/body/eval_jaxpr/rgkt,rgkad->tad/dot_general | solution.py:53
  268.6 3.1 constant_dynamic-slice_fusion.9
  271.7 2.6 reshape.58
  277.8 4.5 fusion.61
  282.3 14.6 %fusion.63 = f32[4,128,128]{2,0,1:T(4,128)S(1)} fusion(f32[4,4,8,128,128]{4,3,2,1,0:T(8,128)} %fusion.61, f32[4,128,128]{2,0,1:T(4,128)S(1)} %get-tuple-element.418, pred[]{:T(512)S(6)} %compare.3, f32[4,4,8]{2,0,1:T(4,128)S(1)} %fusion.62, s32[4,4,8]{2,0,1:T(4,128)S(1)} %get-tuple-element.402), kind=kOutput, calls=%fused_computation.14.clone.1 | convolution fusion | flops 100795392 | bytes 8913921 | tf_op jit(solution)/shard_map/while/body/eval_jaxpr/rgkt,rgkad->tad/dot_general | solution.py:53
  297.0 3.1 constant_dynamic-slice_fusion.9
  300.1 2.6 reshape.58
  306.2 4.5 fusion.61
  310.7 14.6 %fusion.63 = f32[4,128,128]{2,0,1:T(4,128)S(1)} fusion(f32[4,4,8,128,128]{4,3,2,1,0:T(8,128)} %fusion.61, f32[4,128,128]{2,0,1:T(4,128)S(1)} %get-tuple-element.418, pred[]{:T(512)S(6)} %compare.3, f32[4,4,8]{2,0,1:T(4,128)S(1)} %fusion.62, s32[4,4,8]{2,0,1:T(4,128)S(1)} %get-tuple-element.402), kind=kOutput, calls=%fused_computation.14.clone.1 | convolution fusion | flops 100795392 | bytes 8913921 | tf_op jit(solution)/shard_map/while/body/eval_jaxpr/rgkt,rgkad->tad/dot_general | solution.py:53
  325.4 3.1 constant_dynamic-slice_fusion.9
  328.4 2.6 reshape.58
  334.5 4.5 fusion.61
  339.1 14.6 %fusion.63 = f32[4,128,128]{2,0,1:T(4,128)S(1)} fusion(f32[4,4,8,128,128]{4,3,2,1,0:T(8,128)} %fusion.61, f32[4,128,128]{2,0,1:T(4,128)S(1)} %get-tuple-element.418, pred[]{:T(512)S(6)} %compare.3, f32[4,4,8]{2,0,1:T(4,128)S(1)} %fusion.62, s32[4,4,8]{2,0,1:T(4,128)S(1)} %get-tuple-element.402), kind=kOutput, calls=%fused_computation.14.clone.1 | convolution fusion | flops 100795392 | bytes 8913921 | tf_op jit(solution)/shard_map/while/body/eval_jaxpr/rgkt,rgkad->tad/dot_general | solution.py:53
  353.7 3.1 constant_dynamic-slice_fusion.9
  356.8 2.6 reshape.58
  362.9 4.5 fusion.61
  367.5 14.6 %fusion.63 = f32[4,128,128]{2,0,1:T(4,128)S(1)} fusion(f32[4,4,8,128,128]{4,3,2,1,0:T(8,128)} %fusion.61, f32[4,128,128]{2,0,1:T(4,128)S(1)} %get-tuple-element.418, pred[]{:T(512)S(6)} %compare.3, f32[4,4,8]{2,0,1:T(4,128)S(1)} %fusion.62, s32[4,4,8]{2,0,1:T(4,128)S(1)} %get-tuple-element.402), kind=kOutput, calls=%fused_computation.14.clone.1 | convolution fusion | flops 100795392 | bytes 8913921 | tf_op jit(solution)/shard_map/while/body/eval_jaxpr/rgkt,rgkad->tad/dot_general | solution.py:53
  382.1 3.1 constant_dynamic-slice_fusion.9
  385.2 2.6 reshape.58
  391.3 4.5 fusion.61
  395.8 14.6 %fusion.63 = f32[4,128,128]{2,0,1:T(4,128)S(1)} fusion(f32[4,4,8,128,128]{4,3,2,1,0:T(8,128)} %fusion.61, f32[4,128,128]{2,0,1:T(4,128)S(1)} %get-tuple-element.418, pred[]{:T(512)S(6)} %compare.3, f32[4,4,8]{2,0,1:T(4,128)S(1)} %fusion.62, s32[4,4,8]{2,0,1:T(4,128)S(1)} %get-tuple-element.402), kind=kOutput, calls=%fused_computation.14.clone.1 | convolution fusion | flops 100795392 | bytes 8913921 | tf_op jit(solution)/shard_map/while/body/eval_jaxpr/rgkt,rgkad->tad/dot_general | solution.py:53
  410.5 3.1 constant_dynamic-slice_fusion.9
  413.5 2.6 reshape.58
  419.7 4.5 fusion.61
  424.2 14.6 %fusion.63 = f32[4,128,128]{2,0,1:T(4,128)S(1)} fusion(f32[4,4,8,128,128]{4,3,2,1,0:T(8,128)} %fusion.61, f32[4,128,128]{2,0,1:T(4,128)S(1)} %get-tuple-element.418, pred[]{:T(512)S(6)} %compare.3, f32[4,4,8]{2,0,1:T(4,128)S(1)} %fusion.62, s32[4,4,8]{2,0,1:T(4,128)S(1)} %get-tuple-element.402), kind=kOutput, calls=%fused_computation.14.clone.1 | convolution fusion | flops 100795392 | bytes 8913921 | tf_op jit(solution)/shard_map/while/body/eval_jaxpr/rgkt,rgkad->tad/dot_general | solution.py:53
  438.8 3.1 constant_dynamic-slice_fusion.9
  441.9 2.6 reshape.58
  448.0 4.5 fusion.61
  452.6 14.6 %fusion.63 = f32[4,128,128]{2,0,1:T(4,128)S(1)} fusion(f32[4,4,8,128,128]{4,3,2,1,0:T(8,128)} %fusion.61, f32[4,128,128]{2,0,1:T(4,128)S(1)} %get-tuple-element.418, pred[]{:T(512)S(6)} %compare.3, f32[4,4,8]{2,0,1:T(4,128)S(1)} %fusion.62, s32[4,4,8]{2,0,1:T(4,128)S(1)} %get-tuple-element.402), kind=kOutput, calls=%fused_computation.14.clone.1 | convolution fusion | flops 100795392 | bytes 8913921 | tf_op jit(solution)/shard_map/while/body/eval_jaxpr/rgkt,rgkad->tad/dot_general | solution.py:53
  467.2 3.1 constant_dynamic-slice_fusion.9
  470.3 2.6 reshape.58
  476.4 4.5 fusion.61
  480.9 14.6 %fusion.63 = f32[4,128,128]{2,0,1:T(4,128)S(1)} fusion(f32[4,4,8,128,128]{4,3,2,1,0:T(8,128)} %fusion.61, f32[4,128,128]{2,0,1:T(4,128)S(1)} %get-tuple-element.418, pred[]{:T(512)S(6)} %compare.3, f32[4,4,8]{2,0,1:T(4,128)S(1)} %fusion.62, s32[4,4,8]{2,0,1:T(4,128)S(1)} %get-tuple-element.402), kind=kOutput, calls=%fused_computation.14.clone.1 | convolution fusion | flops 100795392 | bytes 8913921 | tf_op jit(solution)/shard_map/while/body/eval_jaxpr/rgkt,rgkad->tad/dot_general | solution.py:53
  495.6 3.1 constant_dynamic-slice_fusion.9
  498.6 2.6 reshape.58
  504.8 4.5 fusion.61
  509.3 14.6 %fusion.63 = f32[4,128,128]{2,0,1:T(4,128)S(1)} fusion(f32[4,4,8,128,128]{4,3,2,1,0:T(8,128)} %fusion.61, f32[4,128,128]{2,0,1:T(4,128)S(1)} %get-tuple-element.418, pred[]{:T(512)S(6)} %compare.3, f32[4,4,8]{2,0,1:T(4,128)S(1)} %fusion.62, s32[4,4,8]{2,0,1:T(4,128)S(1)} %get-tuple-element.402), kind=kOutput, calls=%fused_computation.14.clone.1 | convolution fusion | flops 100795392 | bytes 8913921 | tf_op jit(solution)/shard_map/while/body/eval_jaxpr/rgkt,rgkad->tad/dot_general | solution.py:53
  524.0 3.1 constant_dynamic-slice_fusion.9
  533.1 4.5 fusion.61
  537.7 14.6 %fusion.63 = f32[4,128,128]{2,0,1:T(4,128)S(1)} fusion(f32[4,4,8,128,128]{4,3,2,1,0:T(8,128)} %fusion.61, f32[4,128,128]{2,0,1:T(4,128)S(1)} %get-tuple-element.418, pred[]{:T(512)S(6)} %compare.3, f32[4,4,8]{2,0,1:T(4,128)S(1)} %fusion.62, s32[4,4,8]{2,0,1:T(4,128)S(1)} %get-tuple-element.402), kind=kOutput, calls=%fused_computation.14.clone.1 | convolution fusion | flops 100795392 | bytes 8913921 | tf_op jit(solution)/shard_map/while/body/eval_jaxpr/rgkt,rgkad->tad/dot_general | solution.py:53
  552.3 3.1 constant_dynamic-slice_fusion.9
  561.5 4.5 fusion.61
  566.0 14.6 %fusion.63 = f32[4,128,128]{2,0,1:T(4,128)S(1)} fusion(f32[4,4,8,128,128]{4,3,2,1,0:T(8,128)} %fusion.61, f32[4,128,128]{2,0,1:T(4,128)S(1)} %get-tuple-element.418, pred[]{:T(512)S(6)} %compare.3, f32[4,4,8]{2,0,1:T(4,128)S(1)} %fusion.62, s32[4,4,8]{2,0,1:T(4,128)S(1)} %get-tuple-element.402), kind=kOutput, calls=%fused_computation.14.clone.1 | convolution fusion | flops 100795392 | bytes 8913921 | tf_op jit(solution)/shard_map/while/body/eval_jaxpr/rgkt,rgkad->tad/dot_general | solution.py:53
  580.7 3.1 constant_dynamic-slice_fusion.9
  589.9 4.5 fusion.61
  594.4 14.6 %fusion.63 = f32[4,128,128]{2,0,1:T(4,128)S(1)} fusion(f32[4,4,8,128,128]{4,3,2,1,0:T(8,128)} %fusion.61, f32[4,128,128]{2,0,1:T(4,128)S(1)} %get-tuple-element.418, pred[]{:T(512)S(6)} %compare.3, f32[4,4,8]{2,0,1:T(4,128)S(1)} %fusion.62, s32[4,4,8]{2,0,1:T(4,128)S(1)} %get-tuple-element.402), kind=kOutput, calls=%fused_computation.14.clone.1 | convolution fusion | flops 100795392 | bytes 8913921 | tf_op jit(solution)/shard_map/while/body/eval_jaxpr/rgkt,rgkad->tad/dot_general | solution.py:53
  609.1 3.1 constant_dynamic-slice_fusion.9
  618.2 4.5 fusion.61
  622.8 14.6 %fusion.63 = f32[4,128,128]{2,0,1:T(4,128)S(1)} fusion(f32[4,4,8,128,128]{4,3,2,1,0:T(8,128)} %fusion.61, f32[4,128,128]{2,0,1:T(4,128)S(1)} %get-tuple-element.418, pred[]{:T(512)S(6)} %compare.3, f32[4,4,8]{2,0,1:T(4,128)S(1)} %fusion.62, s32[4,4,8]{2,0,1:T(4,128)S(1)} %get-tuple-element.402), kind=kOutput, calls=%fused_computation.14.clone.1 | convolution fusion | flops 100795392 | bytes 8913921 | tf_op jit(solution)/shard_map/while/body/eval_jaxpr/rgkt,rgkad->tad/dot_general | solution.py:53
  637.4 3.1 constant_dynamic-slice_fusion.9
  646.6 4.5 fusion.61
  651.2 14.6 %fusion.63 = f32[4,128,128]{2,0,1:T(4,128)S(1)} fusion(f32[4,4,8,128,128]{4,3,2,1,0:T(8,128)} %fusion.61, f32[4,128,128]{2,0,1:T(4,128)S(1)} %get-tuple-element.418, pred[]{:T(512)S(6)} %compare.3, f32[4,4,8]{2,0,1:T(4,128)S(1)} %fusion.62, s32[4,4,8]{2,0,1:T(4,128)S(1)} %get-tuple-element.402), kind=kOutput, calls=%fused_computation.14.clone.1 | convolution fusion | flops 100795392 | bytes 8913921 | tf_op jit(solution)/shard_map/while/body/eval_jaxpr/rgkt,rgkad->tad/dot_general | solution.py:53
  666.5 31.5 %all-reduce.2.cloned.1.call-done = f32[512,128]{1,0:T(8,128)} async-done(((f32[512,128]{1,0:T(8,128)}), f32[512,128]{1,0:T(8,128)}) %all-reduce.2.cloned.1.call-update) | async-done | bytes 262160 | tf_op jit(solution)/shard_map/psum | solution.py:77
  (160 shorter events, 75.9 us)
Async XLA Ops:
  6.5 1.0 copy-start
  6.5 205.3 %all-gather.2.cloned.1.call-start = ((), (), s32[]{:S(2)}) async-start(), calls=%async_computation.1 | async-start | bytes 34078720 | tf_op jit(solution)/shard_map/all_gather | solution.py:62
  22.9 675.1 %all-reduce.2.cloned.1.call-start = ((), (), s32[]{:S(2)}) async-start(), calls=%async_computation.2 | async-start | bytes 524288 | tf_op jit(solution)/shard_map/psum | solution.py:77
  22.9 7.4 %copy-start.4 = (s32[4,1,64,8]{2,3,1,0:T(8,128)S(1)}, s32[4,1,64,8]{2,3,1,0:T(8,128)}, u32[]{:S(2)}) copy-start(s32[4,1,64,8]{2,3,1,0:T(8,128)} %param.13) | copy-start | bytes 24580
  23.0 7.5 %copy-start.5 = (s32[4,1,64,8]{2,3,1,0:T(8,128)S(1)}, s32[4,1,64,8]{2,3,1,0:T(8,128)}, u32[]{:S(2)}) copy-start(s32[4,1,64,8]{2,3,1,0:T(8,128)} %param.15) | copy-start | bytes 24580
  23.0 7.6 %copy-start.6 = (s32[4,1,64,8]{2,3,1,0:T(8,128)S(1)}, s32[4,1,64,8]{2,3,1,0:T(8,128)}, u32[]{:S(2)}) copy-start(s32[4,1,64,8]{2,3,1,0:T(8,128)} %param.14) | copy-start | bytes 24580
  23.0 7.7 %copy-start.7 = (s32[4,1,64]{2,1,0:T(1,128)S(1)}, s32[4,1,64]{2,1,0:T(1,128)}, u32[]{:S(2)}) copy-start(s32[4,1,64]{2,1,0:T(1,128)} %param.16) | copy-start | bytes 3076
  211.8 486.1 %copy-start.2 = (bf16[1,1,256,128]{3,2,1,0:T(8,128)(2,1)S(1)}, bf16[1,1,256,128]{3,2,1,0:T(8,128)(2,1)}, u32[]{:S(2)}) copy-start(bf16[1,1,256,128]{3,2,1,0:T(8,128)(2,1)} %param.10) | copy-start | bytes 196612
  211.9 486.1 %copy-start.3 = (bf16[128,128]{1,0:T(8,128)(2,1)S(1)}, bf16[128,128]{1,0:T(8,128)(2,1)}, u32[]{:S(2)}) copy-start(bf16[128,128]{1,0:T(8,128)(2,1)} %param.12) | copy-start | bytes 98308
  217.6 2.2 copy-start.1
  245.9 2.2 copy-start.1
  274.3 2.2 copy-start.1
  302.7 2.2 copy-start.1
  331.1 2.2 copy-start.1
  359.4 2.2 copy-start.1
  387.8 2.2 copy-start.1
  416.2 2.2 copy-start.1
  444.5 2.2 copy-start.1
  472.9 2.2 copy-start.1
  501.3 2.2 copy-start.1
  529.6 2.2 copy-start.1
  558.0 2.2 copy-start.1
  586.4 2.2 copy-start.1
  614.8 2.2 copy-start.1
  643.1 2.2 copy-start.1
Sparse Core Ops, SparseCore 0:
  23.0 188.7 all-gather.1
  666.6 31.2 all-reduce.1
where the time goes:
time: 709 us; the launch traced here: 706 us
  matrix products  357 us (50%)
  waiting for transfers between devices  213 us (30%)
  local copies, waits for them, and re-layouts  108 us (15%)
  between operations  13.5 us (2%)
  blocking collectives  13.2 us (2%)
    dot_general x16, matrix products, apply_group(): jnp.einsum('rgkt,rgkad->tad', onehot, product, precision=lax.Precision.HI...  233 us
    all_gather x1, waiting for transfers between devices, shards(): piece = lax.all_gather(mine, 'blk', axis=1, tiled=True)  181 us
    dot_general x16, matrix products, apply_group(): jnp.einsum('rgkab,rgkbd->rgkad', weights, picked, preferred_element_type=...  71.4 us
    dynamic_slice x16, local copies, waits for them, and re-layouts, fetch(): lax.dynamic_slice_in_dim(piece, offset * block_rows, group * block_rows, 1)  49 us
    reshape x16, local copies, waits for them, and re-layouts, apply_group(): hidden_group.reshape(rel_dev, group, tiles_block, tile_size * width)  42 us
    psum x1, waiting for transfers between devices, shards(): summed = lax.psum(partial_rows, 'chan')  31.5 us
    dot_general x16, matrix products, apply_group(): jnp.einsum('rgks,rgsx->rgkx', pick_cols, flat_hidden, preferred_element_t...  28.2 us
    dot_general x16, matrix products, apply_group(): jnp.einsum('rgkp,rpx->rgkx', pick_ids, pool_flat, preferred_element_type=...  20.7 us
  transfers between devices with their start and end apart: 2, of which 2 were waited for; matrix products, arithmetic and copies ran while one was open for 1% of the time, Pallas kernels for 0%

commit v1 on v0

--- a/solution.py
+++ b/solution.py
@@ -74,7 +74,7 @@
 
     agg = lax.fori_loop(0, turns, step_once, empty)
     partial_rows = agg.reshape(block_rows, width)
-    summed = lax.psum(partial_rows, "chan")
+    summed = jnp.sum(lax.all_gather(partial_rows, "chan"), axis=0)
     share = lax.dynamic_slice_in_dim(summed, chan_index * half_rows, half_rows, 0)
     selfterm = jnp.dot(own_rows, self_weight, preferred_element_type=jnp.float32)
     updated = jax.nn.relu(selfterm + share).astype(jnp.bfloat16)

time: 709 us -> 686 us (0.968)
  waiting for transfers between devices: 213 us -> 181 us
  blocking collectives: 13.2 us -> 23 us
    psum x1 -> x0, waiting for transfers between devices: 31.5 us -> none  [shards(): summed = lax.psum(partial_rows, 'chan')]
    all_gather x0 -> x1, blocking collectives: none -> 9.81 us  [shards(): summed = jnp.sum(lax.all_gather(partial_rows, 'chan'), axis=0)]
  transfers between devices with their start and end apart: 2 -> 1, of which waited for: 2 -> 1; matrix products, arithmetic and copies ran while one was open for 1% -> 1% of each run, Pallas kernels for 0% -> 0%
where the time goes in v1:
time: 686 us; the launch traced here: 683 us
  matrix products  356 us (52%)
  waiting for transfers between devices  181 us (26%)
  local copies, waits for them, and re-layouts  108 us (16%)
  blocking collectives  23 us (3%)
  between operations  13.5 us (2%)
    dot_general x16, matrix products, apply_group(): jnp.einsum('rgkt,rgkad->tad', onehot, product, precision=lax.Precision.HI...  233 us
    all_gather x1, waiting for transfers between devices, shards(): piece = lax.all_gather(mine, 'blk', axis=1, tiled=True)  181 us
    dot_general x16, matrix products, apply_group(): jnp.einsum('rgkab,rgkbd->rgkad', weights, picked, preferred_element_type=...  71.3 us
    dynamic_slice x16, local copies, waits for them, and re-layouts, fetch(): lax.dynamic_slice_in_dim(piece, offset * block_rows, group * block_rows, 1)  49.2 us
    reshape x16, local copies, waits for them, and re-layouts, apply_group(): hidden_group.reshape(rel_dev, group, tiles_block, tile_size * width)  42 us
    dot_general x16, matrix products, apply_group(): jnp.einsum('rgks,rgsx->rgkx', pick_cols, flat_hidden, preferred_element_t...  28.2 us
    dot_general x16, matrix products, apply_group(): jnp.einsum('rgkp,rpx->rgkx', pick_ids, pool_flat, preferred_element_type=...  20.7 us
  transfers between devices with their start and end apart: 1, of which 1 were waited for; matrix products, arithmetic and copies ran while one was open for 1% of the time, Pallas kernels for 0%

profile of v1, /device:TPU:1, one launch (start us, length us, event | category | flops | bytes accessed | tf_op | source)
XLA Modules:
  0.0 683.5 jit_solution(18112144711508040818)
XLA Ops:
  8.7 13.2 %all_to_all.18 = bf16[8,256,128]{1,2,0:T(8,128)(2,1)S(1)} all-to-all(bf16[8,256,128]{1,2,0:T(8,128)(2,1)S(1)} %fusion.31), channel_id=1, replica_groups=mesh['chan'=2,'blk'=64] {'chan'}, dimensions={0} | all-to-all | bytes 1048576 | tf_op jit(solution)/shard_map/all_to_all | solution.py:61
  23.0 7.3 %reshape_squeeze.3 = bf16[4,32,16384]{2,1,0:T(8,128)(2,1)} reshape(bf16[4,1,32,128,128]{4,3,2,1,0:T(8,128)(2,1)} %param.17) | data formatting | bytes 8388608 | tf_op jit(solution)/shard_map/reshape;squeeze | solution.py:26
  30.7 181.1 %all-gather.2.cloned.1.call-done = bf16[4,32768,128]{2,1,0:T(8,128)(2,1)} async-done(((bf16[4,512,128]{2,1,0:T(8,128)(2,1)}), bf16[4,32768,128]{2,1,0:T(8,128)(2,1)}) %all-gather.2.cloned.1.call-update) | async-done | bytes 33554448 | tf_op jit(solution)/shard_map/all_gather | solution.py:62
  211.9 454.1 %while.17 = (s32[]{:T(128)}, f32[4,128,128]{2,0,1:T(4,128)S(1)}, s32[4,64,8]{2,0,1:T(4,128)S(1)}, s32[4,64]{0,1:T(8,128)S(1)}, s32[4,64,8]{2,1,0:T(8,128)S(1)}, ...) while((s32[]{:T(128)}, f32[4,128,128]{2,0,1:T(4,128)S(1)}, ...), condition=%wide.region_1.0_spmd.clone.clone, body=%wide.region_0.0_spmd.clone.clone.sunk | while | flops 792860416 | bytes 65542100 | solution.py:75
  211.9 3.1 constant_dynamic-slice_fusion.9
  215.0 2.6 reshape.54
  221.1 4.5 fusion.61
  225.6 14.6 %fusion.63 = f32[4,128,128]{2,0,1:T(4,128)S(1)} fusion(f32[4,4,8,128,128]{4,3,2,1,0:T(8,128)} %fusion.61, f32[4,128,128]{2,0,1:T(4,128)S(1)} %get-tuple-element.418, pred[]{:T(512)S(6)} %compare.3, f32[4,4,8]{2,0,1:T(4,128)S(1)} %fusion.62, s32[4,4,8]{2,0,1:T(4,128)S(1)} %get-tuple-element.402), kind=kOutput, calls=%fused_computation.14.clone.1 | convolution fusion | flops 100795392 | bytes 8913921 | tf_op jit(solution)/shard_map/while/body/eval_jaxpr/rgkt,rgkad->tad/dot_general | solution.py:53
  240.3 3.1 constant_dynamic-slice_fusion.9
  243.3 2.6 reshape.54
  249.5 4.5 fusion.61
  254.0 14.6 %fusion.63 = f32[4,128,128]{2,0,1:T(4,128)S(1)} fusion(f32[4,4,8,128,128]{4,3,2,1,0:T(8,128)} %fusion.61, f32[4,128,128]{2,0,1:T(4,128)S(1)} %get-tuple-element.418, pred[]{:T(512)S(6)} %compare.3, f32[4,4,8]{2,0,1:T(4,128)S(1)} %fusion.62, s32[4,4,8]{2,0,1:T(4,128)S(1)} %get-tuple-element.402), kind=kOutput, calls=%fused_computation.14.clone.1 | convolution fusion | flops 100795392 | bytes 8913921 | tf_op jit(solution)/shard_map/while/body/eval_jaxpr/rgkt,rgkad->tad/dot_general | solution.py:53
  268.7 3.1 constant_dynamic-slice_fusion.9
  271.7 2.6 reshape.54
  277.9 4.5 fusion.61
  282.4 14.6 %fusion.63 = f32[4,128,128]{2,0,1:T(4,128)S(1)} fusion(f32[4,4,8,128,128]{4,3,2,1,0:T(8,128)} %fusion.61, f32[4,128,128]{2,0,1:T(4,128)S(1)} %get-tuple-element.418, pred[]{:T(512)S(6)} %compare.3, f32[4,4,8]{2,0,1:T(4,128)S(1)} %fusion.62, s32[4,4,8]{2,0,1:T(4,128)S(1)} %get-tuple-element.402), kind=kOutput, calls=%fused_computation.14.clone.1 | convolution fusion | flops 100795392 | bytes 8913921 | tf_op jit(solution)/shard_map/while/body/eval_jaxpr/rgkt,rgkad->tad/dot_general | solution.py:53
  297.0 3.1 constant_dynamic-slice_fusion.9
  300.1 2.6 reshape.54
  306.2 4.5 fusion.61
  310.8 14.6 %fusion.63 = f32[4,128,128]{2,0,1:T(4,128)S(1)} fusion(f32[4,4,8,128,128]{4,3,2,1,0:T(8,128)} %fusion.61, f32[4,128,128]{2,0,1:T(4,128)S(1)} %get-tuple-element.418, pred[]{:T(512)S(6)} %compare.3, f32[4,4,8]{2,0,1:T(4,128)S(1)} %fusion.62, s32[4,4,8]{2,0,1:T(4,128)S(1)} %get-tuple-element.402), kind=kOutput, calls=%fused_computation.14.clone.1 | convolution fusion | flops 100795392 | bytes 8913921 | tf_op jit(solution)/shard_map/while/body/eval_jaxpr/rgkt,rgkad->tad/dot_general | solution.py:53
  325.4 3.1 constant_dynamic-slice_fusion.9
  328.5 2.6 reshape.54
  334.6 4.5 fusion.61
  339.2 14.6 %fusion.63 = f32[4,128,128]{2,0,1:T(4,128)S(1)} fusion(f32[4,4,8,128,128]{4,3,2,1,0:T(8,128)} %fusion.61, f32[4,128,128]{2,0,1:T(4,128)S(1)} %get-tuple-element.418, pred[]{:T(512)S(6)} %compare.3, f32[4,4,8]{2,0,1:T(4,128)S(1)} %fusion.62, s32[4,4,8]{2,0,1:T(4,128)S(1)} %get-tuple-element.402), kind=kOutput, calls=%fused_computation.14.clone.1 | convolution fusion | flops 100795392 | bytes 8913921 | tf_op jit(solution)/shard_map/while/body/eval_jaxpr/rgkt,rgkad->tad/dot_general | solution.py:53
  353.8 3.1 constant_dynamic-slice_fusion.9
  356.9 2.6 reshape.54
  363.0 4.5 fusion.61
  367.5 14.6 %fusion.63 = f32[4,128,128]{2,0,1:T(4,128)S(1)} fusion(f32[4,4,8,128,128]{4,3,2,1,0:T(8,128)} %fusion.61, f32[4,128,128]{2,0,1:T(4,128)S(1)} %get-tuple-element.418, pred[]{:T(512)S(6)} %compare.3, f32[4,4,8]{2,0,1:T(4,128)S(1)} %fusion.62, s32[4,4,8]{2,0,1:T(4,128)S(1)} %get-tuple-element.402), kind=kOutput, calls=%fused_computation.14.clone.1 | convolution fusion | flops 100795392 | bytes 8913921 | tf_op jit(solution)/shard_map/while/body/eval_jaxpr/rgkt,rgkad->tad/dot_general | solution.py:53
  382.2 3.1 constant_dynamic-slice_fusion.9
  385.3 2.6 reshape.54
  391.4 4.5 fusion.61
  395.9 14.6 %fusion.63 = f32[4,128,128]{2,0,1:T(4,128)S(1)} fusion(f32[4,4,8,128,128]{4,3,2,1,0:T(8,128)} %fusion.61, f32[4,128,128]{2,0,1:T(4,128)S(1)} %get-tuple-element.418, pred[]{:T(512)S(6)} %compare.3, f32[4,4,8]{2,0,1:T(4,128)S(1)} %fusion.62, s32[4,4,8]{2,0,1:T(4,128)S(1)} %get-tuple-element.402), kind=kOutput, calls=%fused_computation.14.clone.1 | convolution fusion | flops 100795392 | bytes 8913921 | tf_op jit(solution)/shard_map/while/body/eval_jaxpr/rgkt,rgkad->tad/dot_general | solution.py:53
  410.6 3.1 constant_dynamic-slice_fusion.9
  413.6 2.6 reshape.54
  419.8 4.5 fusion.61
  424.3 14.6 %fusion.63 = f32[4,128,128]{2,0,1:T(4,128)S(1)} fusion(f32[4,4,8,128,128]{4,3,2,1,0:T(8,128)} %fusion.61, f32[4,128,128]{2,0,1:T(4,128)S(1)} %get-tuple-element.418, pred[]{:T(512)S(6)} %compare.3, f32[4,4,8]{2,0,1:T(4,128)S(1)} %fusion.62, s32[4,4,8]{2,0,1:T(4,128)S(1)} %get-tuple-element.402), kind=kOutput, calls=%fused_computation.14.clone.1 | convolution fusion | flops 100795392 | bytes 8913921 | tf_op jit(solution)/shard_map/while/body/eval_jaxpr/rgkt,rgkad->tad/dot_general | solution.py:53
  438.9 3.1 constant_dynamic-slice_fusion.9
  442.0 2.6 reshape.54
  448.1 4.5 fusion.61
  452.7 14.6 %fusion.63 = f32[4,128,128]{2,0,1:T(4,128)S(1)} fusion(f32[4,4,8,128,128]{4,3,2,1,0:T(8,128)} %fusion.61, f32[4,128,128]{2,0,1:T(4,128)S(1)} %get-tuple-element.418, pred[]{:T(512)S(6)} %compare.3, f32[4,4,8]{2,0,1:T(4,128)S(1)} %fusion.62, s32[4,4,8]{2,0,1:T(4,128)S(1)} %get-tuple-element.402), kind=kOutput, calls=%fused_computation.14.clone.1 | convolution fusion | flops 100795392 | bytes 8913921 | tf_op jit(solution)/shard_map/while/body/eval_jaxpr/rgkt,rgkad->tad/dot_general | solution.py:53
  467.3 3.1 constant_dynamic-slice_fusion.9
  470.4 2.6 reshape.54
  476.5 4.5 fusion.61
  481.1 14.6 %fusion.63 = f32[4,128,128]{2,0,1:T(4,128)S(1)} fusion(f32[4,4,8,128,128]{4,3,2,1,0:T(8,128)} %fusion.61, f32[4,128,128]{2,0,1:T(4,128)S(1)} %get-tuple-element.418, pred[]{:T(512)S(6)} %compare.3, f32[4,4,8]{2,0,1:T(4,128)S(1)} %fusion.62, s32[4,4,8]{2,0,1:T(4,128)S(1)} %get-tuple-element.402), kind=kOutput, calls=%fused_computation.14.clone.1 | convolution fusion | flops 100795392 | bytes 8913921 | tf_op jit(solution)/shard_map/while/body/eval_jaxpr/rgkt,rgkad->tad/dot_general | solution.py:53
  495.7 3.1 constant_dynamic-slice_fusion.9
  504.9 4.5 fusion.61
  509.4 14.6 %fusion.63 = f32[4,128,128]{2,0,1:T(4,128)S(1)} fusion(f32[4,4,8,128,128]{4,3,2,1,0:T(8,128)} %fusion.61, f32[4,128,128]{2,0,1:T(4,128)S(1)} %get-tuple-element.418, pred[]{:T(512)S(6)} %compare.3, f32[4,4,8]{2,0,1:T(4,128)S(1)} %fusion.62, s32[4,4,8]{2,0,1:T(4,128)S(1)} %get-tuple-element.402), kind=kOutput, calls=%fused_computation.14.clone.1 | convolution fusion | flops 100795392 | bytes 8913921 | tf_op jit(solution)/shard_map/while/body/eval_jaxpr/rgkt,rgkad->tad/dot_general | solution.py:53
  524.1 3.1 constant_dynamic-slice_fusion.9
  533.3 4.5 fusion.61
  537.8 14.6 %fusion.63 = f32[4,128,128]{2,0,1:T(4,128)S(1)} fusion(f32[4,4,8,128,128]{4,3,2,1,0:T(8,128)} %fusion.61, f32[4,128,128]{2,0,1:T(4,128)S(1)} %get-tuple-element.418, pred[]{:T(512)S(6)} %compare.3, f32[4,4,8]{2,0,1:T(4,128)S(1)} %fusion.62, s32[4,4,8]{2,0,1:T(4,128)S(1)} %get-tuple-element.402), kind=kOutput, calls=%fused_computation.14.clone.1 | convolution fusion | flops 100795392 | bytes 8913921 | tf_op jit(solution)/shard_map/while/body/eval_jaxpr/rgkt,rgkad->tad/dot_general | solution.py:53
  552.5 3.1 constant_dynamic-slice_fusion.9
  555.5 2.6 reshape.54
  561.7 4.5 fusion.61
  566.2 14.6 %fusion.63 = f32[4,128,128]{2,0,1:T(4,128)S(1)} fusion(f32[4,4,8,128,128]{4,3,2,1,0:T(8,128)} %fusion.61, f32[4,128,128]{2,0,1:T(4,128)S(1)} %get-tuple-element.418, pred[]{:T(512)S(6)} %compare.3, f32[4,4,8]{2,0,1:T(4,128)S(1)} %fusion.62, s32[4,4,8]{2,0,1:T(4,128)S(1)} %get-tuple-element.402), kind=kOutput, calls=%fused_computation.14.clone.1 | convolution fusion | flops 100795392 | bytes 8913921 | tf_op jit(solution)/shard_map/while/body/eval_jaxpr/rgkt,rgkad->tad/dot_general | solution.py:53
  580.8 3.1 constant_dynamic-slice_fusion.9
  590.0 4.5 fusion.61
  594.6 14.6 %fusion.63 = f32[4,128,128]{2,0,1:T(4,128)S(1)} fusion(f32[4,4,8,128,128]{4,3,2,1,0:T(8,128)} %fusion.61, f32[4,128,128]{2,0,1:T(4,128)S(1)} %get-tuple-element.418, pred[]{:T(512)S(6)} %compare.3, f32[4,4,8]{2,0,1:T(4,128)S(1)} %fusion.62, s32[4,4,8]{2,0,1:T(4,128)S(1)} %get-tuple-element.402), kind=kOutput, calls=%fused_computation.14.clone.1 | convolution fusion | flops 100795392 | bytes 8913921 | tf_op jit(solution)/shard_map/while/body/eval_jaxpr/rgkt,rgkad->tad/dot_general | solution.py:53
  609.2 3.1 constant_dynamic-slice_fusion.9
  618.4 4.5 fusion.61
  623.0 14.6 %fusion.63 = f32[4,128,128]{2,0,1:T(4,128)S(1)} fusion(f32[4,4,8,128,128]{4,3,2,1,0:T(8,128)} %fusion.61, f32[4,128,128]{2,0,1:T(4,128)S(1)} %get-tuple-element.418, pred[]{:T(512)S(6)} %compare.3, f32[4,4,8]{2,0,1:T(4,128)S(1)} %fusion.62, s32[4,4,8]{2,0,1:T(4,128)S(1)} %get-tuple-element.402), kind=kOutput, calls=%fused_computation.14.clone.1 | convolution fusion | flops 100795392 | bytes 8913921 | tf_op jit(solution)/shard_map/while/body/eval_jaxpr/rgkt,rgkad->tad/dot_general | solution.py:53
  637.6 3.1 constant_dynamic-slice_fusion.9
  646.8 4.5 fusion.61
  651.3 14.6 %fusion.63 = f32[4,128,128]{2,0,1:T(4,128)S(1)} fusion(f32[4,4,8,128,128]{4,3,2,1,0:T(8,128)} %fusion.61, f32[4,128,128]{2,0,1:T(4,128)S(1)} %get-tuple-element.418, pred[]{:T(512)S(6)} %compare.3, f32[4,4,8]{2,0,1:T(4,128)S(1)} %fusion.62, s32[4,4,8]{2,0,1:T(4,128)S(1)} %get-tuple-element.402), kind=kOutput, calls=%fused_computation.14.clone.1 | convolution fusion | flops 100795392 | bytes 8913921 | tf_op jit(solution)/shard_map/while/body/eval_jaxpr/rgkt,rgkad->tad/dot_general | solution.py:53
  666.0 9.8 %all_gather.7 = f32[2,512,128]{2,1,0:T(8,128)S(1)} all-gather(f32[1,512,128]{2,1,0:T(8,128)S(1)} %bitcast.61), channel_id=1, replica_groups=mesh['chan'=2,'blk'=64] {'chan'}, dimensions={0}, use_global_device_ids=true | all-gather | bytes 786432 | tf_op jit(solution)/shard_map/all_gather | solution.py:77
  (159 shorter events, 74.3 us)
Async XLA Ops:
  6.5 1.0 copy-start
  6.5 205.3 %all-gather.2.cloned.1.call-start = ((), (), s32[]{:S(2)}) async-start(), calls=%async_computation.1 | async-start | bytes 34078720 | tf_op jit(solution)/shard_map/all_gather | solution.py:62
  22.9 7.3 %copy-start.4 = (s32[4,1,64,8]{2,3,1,0:T(8,128)S(1)}, s32[4,1,64,8]{2,3,1,0:T(8,128)}, u32[]{:S(2)}) copy-start(s32[4,1,64,8]{2,3,1,0:T(8,128)} %param.13) | copy-start | bytes 24580
  22.9 7.4 %copy-start.5 = (s32[4,1,64,8]{2,3,1,0:T(8,128)S(1)}, s32[4,1,64,8]{2,3,1,0:T(8,128)}, u32[]{:S(2)}) copy-start(s32[4,1,64,8]{2,3,1,0:T(8,128)} %param.15) | copy-start | bytes 24580
  22.9 7.5 %copy-start.6 = (s32[4,1,64,8]{2,3,1,0:T(8,128)S(1)}, s32[4,1,64,8]{2,3,1,0:T(8,128)}, u32[]{:S(2)}) copy-start(s32[4,1,64,8]{2,3,1,0:T(8,128)} %param.14) | copy-start | bytes 24580
  23.0 7.7 %copy-start.7 = (s32[4,1,64]{2,1,0:T(1,128)S(1)}, s32[4,1,64]{2,1,0:T(1,128)}, u32[]{:S(2)}) copy-start(s32[4,1,64]{2,1,0:T(1,128)} %param.16) | copy-start | bytes 3076
  211.9 464.0 %copy-start.2 = (bf16[1,1,256,128]{3,2,1,0:T(8,128)(2,1)S(1)}, bf16[1,1,256,128]{3,2,1,0:T(8,128)(2,1)}, u32[]{:S(2)}) copy-start(bf16[1,1,256,128]{3,2,1,0:T(8,128)(2,1)} %param.10) | copy-start | bytes 196612
  211.9 464.0 %copy-start.3 = (bf16[128,128]{1,0:T(8,128)(2,1)S(1)}, bf16[128,128]{1,0:T(8,128)(2,1)}, u32[]{:S(2)}) copy-start(bf16[128,128]{1,0:T(8,128)(2,1)} %param.12) | copy-start | bytes 98308
  217.6 2.2 copy-start.1
  246.0 2.2 copy-start.1
  274.4 2.2 copy-start.1
  302.8 2.2 copy-start.1
  331.1 2.2 copy-start.1
  359.5 2.2 copy-start.1
  387.9 2.2 copy-start.1
  416.3 2.2 copy-start.1
  444.6 2.2 copy-start.1
  473.0 2.2 copy-start.1
  501.4 2.2 copy-start.1
  529.8 2.2 copy-start.1
  558.2 2.2 copy-start.1
  586.6 2.2 copy-start.1
  614.9 2.2 copy-start.1
  643.3 2.2 copy-start.1
Sparse Core Ops, SparseCore 0:
  23.0 188.7 all-gather.1
